TPU v7x, 256 devices: a whole 4x4x8 slice. The times are simulated.
256 devices in a mesh: ent: 64 (over x, z, core), rel: 4 (over y).
Axes of the slice: x: 4, y: 4, z: 8, core: 2. Of those that a mesh axis runs over, the one named last changes fastest.
Arguments:
- state_zero: bfloat16 [65536, 256], P('ent'), may hold values from -6 to 6
- state_one: bfloat16 [65536, 256], P('ent'), may hold values from -6 to 6
- aggregate_one: bfloat16 [65536, 256], P('ent'), may hold values from -6 to 6
- aggregate_two: bfloat16 [65536, 256], P('ent'), may hold values from -6 to 6
- cotangent: bfloat16 [65536, 256], P('ent'), may hold values from -6 to 6
- relation_table: bfloat16 [1312, 256], P('rel'), may hold values from -6 to 6
- update_in: bfloat16 [2, 64, 256], replicated, may hold values from -0.75 to 0.75
- update_bias: float32 [2, 256], replicated, may hold values from -3 to 3
- update_out: bfloat16 [2, 256, 32], replicated, may hold values from -0.375 to 0.375
- frontier_tiles: int32 [2, 128], P(None, 'ent'), may hold values from 0 to 7, as said below
- frontier_count: int32 [2, 64], P(None, 'ent'), may hold values from 1 to 2, as said below
- edge_source: int32 [262144], P(('ent', 'rel')), may hold values from 0 to 1023
- edge_relation: int32 [262144], P(('ent', 'rel')), may hold values from 0 to 327
- edge_target: int32 [262144], P(('ent', 'rel')), may hold values from 0 to 1023
- edge_owner: int32 [262144, 1], P(('ent', 'rel')), may hold values from 0 to 63; in each aligned block of 1024 rows (0 to 1023, 1024 to 2047, ...) at most 24 rows name the same one
Outputs:
- grad_state_zero: bfloat16 [65536, 256], P(('ent', 'rel'))
- grad_relation: float32 [1312, 256], P('rel')
- grad_update_in: float32 [2, 64, 256], replicated
- grad_update_bias: float32 [2, 256], replicated
- grad_update_out: float32 [2, 256, 32], replicated
Inputs may be any that keep to these rules, and one draw needn't show every extreme that they name: `frontier_tiles`: within one owner's 2 slots of a hop the tile numbers are distinct, padded slots included. The first frontier_count entries of an owner's list are its live tiles; in each hop some owner has all 2 live. `edge_owner`: among the 1024 edges of one device at most 24 name the same owner, and in some device some owner is named by exactly 24.
All inputs are finite; a program needn't handle non-finite values.
Results may differ from a plain program's by a relative error of at most 0.009.
Values may be sent and summed in bfloat16 or wider, within the bound.
No kernel may reach another device: no remote copies, remote signals or barrier semaphores. Data moves between devices by JAX's collectives and lax.ppermute only.
A program may use at most 64 MiB of HBM per device.

v0:
```python
import math
import jax
import jax.numpy as jnp
from jax import lax
from jax.sharding import PartitionSpec as P

QUERIES = 8
DIM = 32
TILE = 128


def frontier_rows(tile_ids, live_count, tile_total):
    slot_valid = jnp.arange(tile_ids.shape[0], dtype=jnp.int32) < live_count
    tile_range = jnp.arange(tile_total, dtype=jnp.int32)
    matched = (tile_ids[None, :] == tile_range[:, None]) & slot_valid[None, :]
    return jnp.repeat(jnp.any(matched, axis=1).astype(jnp.float32), TILE)


def exact_pick_sum(selector, values, contract_dim):
    high_part = values.astype(jnp.bfloat16)
    low_part = (values - high_part.astype(jnp.float32)).astype(jnp.bfloat16)
    numbers = (((contract_dim,), (0,)), ((), ()))
    first = lax.dot_general(selector, high_part, numbers, preferred_element_type=jnp.float32)
    second = lax.dot_general(selector, low_part, numbers, preferred_element_type=jnp.float32)
    return first + second


def update_backward(aggregate, state, upstream, update_in, update_bias, update_out):
    row_count = aggregate.shape[0]
    inputs = jnp.concatenate(
        [aggregate.reshape(row_count, QUERIES, DIM), state.reshape(row_count, QUERIES, DIM)], axis=2
    )
    pre_act = (
        jnp.einsum("nqd,de->nqe", inputs, update_in, preferred_element_type=jnp.float32)
        + update_bias
    )
    gate_value = jax.nn.sigmoid(pre_act)
    activated = (pre_act * gate_value).astype(jnp.bfloat16)
    slope = gate_value * (1.0 + pre_act * (1.0 - gate_value))
    upstream_low = upstream.astype(jnp.bfloat16).reshape(row_count, QUERIES, DIM)
    grad_act = jnp.einsum(
        "nqd,ed->nqe", upstream_low, update_out, preferred_element_type=jnp.float32
    )
    grad_pre = grad_act * slope
    grad_pre_low = grad_pre.astype(jnp.bfloat16)
    grad_out = jnp.einsum(
        "nqe,nqd->ed", activated, upstream_low, preferred_element_type=jnp.float32
    )
    grad_bias = jnp.sum(grad_pre, axis=(0, 1))
    grad_in = jnp.einsum("nqd,nqe->de", inputs, grad_pre_low, preferred_element_type=jnp.float32)
    grad_inputs = jnp.einsum(
        "nqe,de->nqd", grad_pre_low, update_in, preferred_element_type=jnp.float32
    )
    grad_agg = grad_inputs[:, :, :DIM].reshape(row_count, QUERIES * DIM).astype(jnp.bfloat16)
    grad_state = grad_inputs[:, :, DIM:].reshape(row_count, QUERIES * DIM)
    return (grad_agg, grad_state, grad_in, grad_bias, grad_out)


def mlp_blocks(aggregate, state, upstream, update_in, update_bias, update_out):
    row_count = aggregate.shape[0]
    feature_width = aggregate.shape[1]
    block_rows = math.gcd(row_count, 512)
    block_count = row_count // block_rows

    def step(carry, pieces):
        grad_agg, grad_state, grad_in, grad_bias, grad_out = update_backward(
            pieces[0], pieces[1], pieces[2], update_in, update_bias, update_out
        )
        return (
            (carry[0] + grad_in, carry[1] + grad_bias, carry[2] + grad_out),
            (grad_agg, grad_state),
        )

    initial = (
        jnp.zeros(update_in.shape, jnp.float32),
        jnp.zeros(update_bias.shape, jnp.float32),
        jnp.zeros(update_out.shape, jnp.float32),
    )
    stacked = tuple(
        (
            source_array.reshape(block_count, block_rows, feature_width)
            for source_array in (aggregate, state, upstream)
        )
    )
    sums, (grad_agg, grad_state) = lax.scan(step, initial, stacked)
    return (
        grad_agg.reshape(row_count, feature_width),
        grad_state.reshape(row_count, feature_width),
        sums,
    )


def shards(
    state_zero,
    state_one,
    aggregate_one,
    aggregate_two,
    cotangent,
    relation_table,
    update_in,
    update_bias,
    update_out,
    frontier_tiles,
    frontier_count,
    edge_source,
    edge_relation,
    edge_target,
    edge_owner,
):
    block_rows = state_zero.shape[0]
    feature_width = state_zero.shape[1]
    group_size = lax.axis_size("rel")
    peer_count = lax.axis_size("ent")
    quarter = block_rows // group_size
    quarter_start = lax.axis_index("rel") * quarter
    edge_count = edge_source.shape[0]
    capacity = 3 * edge_count // (2 * peer_count)
    tile_total = block_rows // TILE
    group_width = relation_table.shape[0]
    edge_peer = edge_owner[:, 0]
    onehot = (edge_peer[:, None] == jnp.arange(peer_count, dtype=jnp.int32)[None, :]).astype(
        jnp.int32
    )
    earlier = jnp.sum((jnp.cumsum(onehot, axis=0) - onehot) * onehot, axis=1)
    edge_slot = edge_peer * capacity + earlier
    request = jnp.zeros((peer_count * capacity,), jnp.int32).at[edge_slot].set(edge_target)
    asked = lax.all_to_all(
        request.reshape(peer_count, capacity), "ent", split_axis=0, concat_axis=0, tiled=True
    )
    source_select = (
        jnp.arange(block_rows, dtype=jnp.int32)[:, None] == edge_source[None, :]
    ).astype(jnp.bfloat16)
    relation_select = (
        edge_relation[:, None] == jnp.arange(group_width, dtype=jnp.int32)[None, :]
    ).astype(jnp.bfloat16)
    edge_table = jnp.dot(relation_select, relation_table, preferred_element_type=jnp.float32)
    upstream = cotangent.astype(jnp.float32)
    relation_grad = jnp.zeros((group_width, feature_width), jnp.float32)
    layer_sums = [None, None]
    for aggregate, state, layer in ((aggregate_two, state_one, 1), (aggregate_one, state_zero, 0)):
        grad_agg, grad_state, sums = mlp_blocks(
            aggregate, state, upstream, update_in[layer], update_bias[layer], update_out[layer]
        )
        picked = grad_agg[asked]
        answered = lax.all_to_all(picked, "ent", split_axis=0, concat_axis=0, tiled=True)
        served = answered.reshape(peer_count * capacity, feature_width)[edge_slot]
        tile_ids = frontier_tiles[layer]
        row_mask = frontier_rows(tile_ids, frontier_count[layer, 0], tile_total)
        weighted = served.astype(jnp.float32) * row_mask[edge_source][:, None]
        contrib = exact_pick_sum(source_select, weighted * edge_table, 1)
        relation_grad = relation_grad + exact_pick_sum(
            relation_select, weighted * state[edge_source].astype(jnp.float32), 0
        )
        source_grad = lax.psum(contrib.astype(jnp.bfloat16), "rel").astype(jnp.float32)
        upstream = upstream + grad_state + source_grad
        layer_sums[layer] = sums
    stacked_in = jnp.stack([layer_sums[0][0], layer_sums[1][0]])
    stacked_bias = jnp.stack([layer_sums[0][1], layer_sums[1][1]])
    stacked_out = jnp.stack([layer_sums[0][2], layer_sums[1][2]])
    grad_in_all, grad_bias_all, grad_out_all, relation_total = lax.psum(
        (stacked_in, stacked_bias, stacked_out, relation_grad), "ent"
    )
    scale_weights = 1.0 / math.sqrt(block_rows * peer_count * QUERIES)
    scale_relations = math.sqrt(group_width * group_size / (edge_count * peer_count * group_size))
    return (
        lax.dynamic_slice_in_dim(upstream, quarter_start, quarter, 0).astype(jnp.bfloat16),
        relation_total * scale_relations,
        grad_in_all * scale_weights,
        grad_bias_all * scale_weights,
        grad_out_all * scale_weights,
    )


def solution(mesh):
    in_specs = (
        P("ent", None),
        P("ent", None),
        P("ent", None),
        P("ent", None),
        P("ent", None),
        P("rel", None),
        P(),
        P(),
        P(),
        P(None, "ent"),
        P(None, "ent"),
        P(("ent", "rel")),
        P(("ent", "rel")),
        P(("ent", "rel")),
        P(("ent", "rel"), None),
    )
    out_specs = (P(("ent", "rel"), None), P("rel", None), P(), P(), P())
    return jax.shard_map(shards, mesh=mesh, in_specs=in_specs, out_specs=out_specs, check_vma=False)
```

profile of v0, /device:TPU:2, one launch (start us, length us, event | category | flops | bytes accessed | tf_op | source)
XLA Modules:
  0.0 626.9 jit_solution(3884639619966283850)
XLA Ops:
  7.9 18.0 %reduce-window.6 = s32[64,8,128]{2,1,0:T(8,128)S(1)} reduce-window(s32[64,8,128]{2,1,0:T(8,128)S(1)} %fusion.77, s32[]{:T(128)} %constant.31.clone.1), window={size=1x1x128 pad=0_0x0_0x127_0}, to_apply=%region_3.4 | reduce-window | flops 8323072 | bytes 524292 | tf_op jit(solution)/shard_map/reduce-window
  28.0 4.5 scatter_custom_fusion
  33.1 12.0 %all-to-all-start = ((s32[64,1,24]{2,1,0:T(1,128)}), s32[64,1,24]{2,1,0:T(1,128)S(1)}, u32[]{:S(2)}, u32[]{:S(2)}) async-start(s32[64,1,24]{2,1,0:T(1,128)} %bitcast.13), calls=%async_computation | async-start | bytes 65536 | tf_op jit(solution)/shard_map/all_to_all | solution.py:127
  49.7 36.1 %while.38 = (s32[]{:T(128)}, f32[64,256]{1,0:T(8,128)S(1)}, f32[256]{0:T(256)S(1)}, f32[256,32]{0,1:T(8,128)S(1)}, bf16[2,512,256]{2,1,0:T(8,128)(2,1)S(1)}, /*i...) while((s32[]{:T(128)}, f32[64,256]{1,0:T(8,128)S(1)}, ...), condition=%wide.region_2.3_spmd.clone, body=%wide.region_0.2_spmd.clone.sunk | while | flops 556843264 | bytes 33839300 | solution.py:85
  55.6 4.0 fusion.123
  73.7 4.0 fusion.123
  86.0 5.4 gather_fusion
  91.4 10.5 %all-to-all-start.1 = ((bf16[64,24,256]{2,1,0:T(8,128)(2,1)}), bf16[64,24,256]{2,1,0:T(8,128)(2,1)S(1)}, u32[]{:S(2)}, u32[]{:S(2)}) async-start(bf16[64,24,256]{2,1,0:T(8,128)(2,1)} %bitcast.15), calls=%async_computation.1 | async-start | bytes 1572864 | tf_op jit(solution)/shard_map/all_to_all | solution.py:145
  104.7 4.5 gather_fusion.2
  109.8 13.9 %all-to-all-done.1 = bf16[64,24,256]{2,1,0:T(8,128)(2,1)S(1)} async-done(((bf16[64,24,256]{2,1,0:T(8,128)(2,1)}), bf16[64,24,256]{2,1,0:T(8,128)(2,1)S(1)}, u32[]{:S(2)}, u32[]{:S(2)}) %all-to-all-start.1) | async-done | bytes 786464 | tf_op jit(solution)/shard_map/all_to_all | solution.py:145
  123.7 3.9 gather_fusion.1
  130.5 46.5 %all-reduce.5.cloned.1.call-done = bf16[1024,256]{1,0:T(8,128)(2,1)} async-done(((bf16[1024,256]{1,0:T(8,128)(2,1)}), bf16[1024,256]{1,0:T(8,128)(2,1)}) %all-reduce.5.cloned.1.call-update) | async-done | bytes 524304 | tf_op jit(solution)/shard_map/psum | solution.py:154
  180.8 35.8 %while.39 = (s32[]{:T(128)}, f32[64,256]{1,0:T(8,128)S(1)}, f32[256]{0:T(256)S(1)}, f32[256,32]{0,1:T(8,128)S(1)}, bf16[2,512,256]{2,1,0:T(8,128)(2,1)S(1)}, /*i...) while((s32[]{:T(128)}, f32[64,256]{1,0:T(8,128)S(1)}, ...), condition=%wide.region_11.12_spmd.clone, body=%wide.region_9.11_spmd.clone.sunk | while | flops 556843264 | bytes 33839300 | solution.py:85
  186.7 4.0 fusion.134
  204.6 4.0 fusion.134
  216.6 5.4 gather_fusion.3
  222.0 10.5 %all-to-all-start.2 = ((bf16[64,24,256]{2,1,0:T(8,128)(2,1)}), bf16[64,24,256]{2,1,0:T(8,128)(2,1)S(1)}, u32[]{:S(2)}, u32[]{:S(2)}) async-start(bf16[64,24,256]{2,1,0:T(8,128)(2,1)} %bitcast.27), calls=%async_computation.2 | async-start | bytes 1572864 | tf_op jit(solution)/shard_map/all_to_all | solution.py:145
  232.8 5.7 gather_fusion.7
  238.5 4.6 gather_fusion.6
  243.3 4.5 gather_fusion.5
  249.5 107.1 %psum.46 = f32[2,256]{1,0:T(2,128)S(1)} all-reduce(f32[2,256]{1,0:T(2,128)S(1)} %pad_maximum_fusion.8), channel_id=1, replica_groups=mesh['ent'=64,'rel'=4] {'ent'}, use_global_device_ids=true, to_apply=%region_16.17 | all-reduce | flops 512 | bytes 4096 | tf_op jit(solution)/shard_map/psum | solution.py:160
  358.4 4.9 gather_fusion.4
  374.4 196.0 %all-reduce.9.cloned.1.call-done = (f32[328,256]{1,0:T(8,128)}, f32[2,64,256]{2,1,0:T(8,128)}, f32[2,256,32]{1,2,0:T(8,128)}) async-done(((f32[328,256]{1,0:T(8,128)}, f32[2,64,256]{2,1,0:T(8,128)}, f32[2,256,32]{1,2,0:T(8,128)}), (f32[328,256]{1,0:T(8,128)}, f32[2,64,256]{2,1,0:T(8,128)}, f32[2,256,32]{1,2,0:T(8,128)})) %all-reduce.9.cloned.1.call-update) | async-done | bytes 532496 | tf_op jit(solution)/shard_map/psum | solution.py:160
  575.1 43.5 %all-reduce.7.cloned.1.call-done = bf16[1024,256]{1,0:T(8,128)(2,1)} async-done(((bf16[1024,256]{1,0:T(8,128)(2,1)}), bf16[1024,256]{1,0:T(8,128)(2,1)}) %all-reduce.7.cloned.1.call-update) | async-done | bytes 524304 | tf_op jit(solution)/shard_map/psum | solution.py:154
  (178 shorter events, 94.9 us)
Async XLA Ops:
  7.2 102.1 %copy-start = (bf16[328,256]{1,0:T(8,128)(2,1)S(1)}, bf16[328,256]{1,0:T(8,128)(2,1)}, u32[]{:S(2)}) copy-start(bf16[328,256]{1,0:T(8,128)(2,1)} %param.24) | copy-start | bytes 503812
  33.1 52.7 %all-to-all-start = ((s32[64,1,24]{2,1,0:T(1,128)}), s32[64,1,24]{2,1,0:T(1,128)S(1)}, u32[]{:S(2)}, u32[]{:S(2)}) async-start(s32[64,1,24]{2,1,0:T(1,128)} %bitcast.13), calls=%async_computation | async-start | bytes 65536 | tf_op jit(solution)/shard_map/all_to_all | solution.py:127
  85.9 5.5 copy-start.11
  86.0 16.1 %copy-start.19 = (s32[2,1]{0,1:T(1,128)S(1)}, s32[2,1]{0,1:T(1,128)}, u32[]{:S(2)}) copy-start(s32[2,1]{0,1:T(1,128)} %param.29) | copy-start | bytes 28
  86.0 18.0 %copy-start.20 = (s32[2,2]{1,0:T(2,128)S(1)}, s32[2,2]{1,0:T(2,128)}, u32[]{:S(2)}) copy-start(s32[2,2]{1,0:T(2,128)} %param.28) | copy-start | bytes 52
  86.0 18.7 %copy-start.15 = (s32[1024]{0:T(1024)S(1)}, s32[1024]{0:T(1024)}, u32[]{:S(2)}) copy-start(s32[1024]{0:T(1024)} %param.30) | copy-start | bytes 12292
  91.4 17.9 %copy-start.13 = (s32[1024]{0:T(1024)S(1)}, s32[1024]{0:T(1024)}, u32[]{:S(2)}) copy-start(s32[1024]{0:T(1024)} %param.31) | copy-start | bytes 12292
  91.4 32.3 %all-to-all-start.1 = ((bf16[64,24,256]{2,1,0:T(8,128)(2,1)}), bf16[64,24,256]{2,1,0:T(8,128)(2,1)S(1)}, u32[]{:S(2)}, u32[]{:S(2)}) async-start(bf16[64,24,256]{2,1,0:T(8,128)(2,1)} %bitcast.15), calls=%async_computation.1 | async-start | bytes 1572864 | tf_op jit(solution)/shard_map/all_to_all | solution.py:145
  101.9 75.2 %all-reduce.5.cloned.1.call-start = ((), (), s32[]{:S(2)}) async-start(), calls=%async_computation.3 | async-start | bytes 1048576 | tf_op jit(solution)/shard_map/psum | solution.py:154
  109.2 19.4 %copy-start.17 = (f32[1024]{0:T(1024)}, f32[1024]{0:T(1024)S(1)}, u32[]{:S(2)}) copy-start(f32[1024]{0:T(1024)S(1)} %gather_fusion.2) | copy-start | bytes 12292
  109.8 18.9 %copy-start.5 = (f32[1024,256]{1,0:T(8,128)}, f32[1024,256]{1,0:T(8,128)S(1)}, u32[]{:S(2)}) copy-start(f32[1024,256]{1,0:T(8,128)S(1)} %fusion.40) | copy-start | bytes 3145732
  127.7 49.4 %copy-start.4 = (f32[2,512,256]{2,1,0:T(8,128)S(1)}, f32[2,512,256]{2,1,0:T(8,128)}, u32[]{:S(2)}) copy-start(f32[2,512,256]{2,1,0:T(8,128)} %get-tuple-element.137) | copy-start | bytes 3145732
  222.0 136.4 %all-to-all-start.2 = ((bf16[64,24,256]{2,1,0:T(8,128)(2,1)}), bf16[64,24,256]{2,1,0:T(8,128)(2,1)S(1)}, u32[]{:S(2)}, u32[]{:S(2)}) async-start(bf16[64,24,256]{2,1,0:T(8,128)(2,1)} %bitcast.27), calls=%async_computation.2 | async-start | bytes 1572864 | tf_op jit(solution)/shard_map/all_to_all | solution.py:145
  232.5 337.8 %all-reduce.9.cloned.1.call-start = ((), (), s32[]{:S(2)}) async-start(), calls=%async_computation.5 | async-start | bytes 1064960 | tf_op jit(solution)/shard_map/psum | solution.py:160
  232.8 10.4 %copy-start.21 = (pred[8]{0:T(512)(128)(4,1)S(1)}, pred[8]{0:T(512)(128)(4,1)}, u32[]{:S(2)}) copy-start(pred[8]{0:T(512)(128)(4,1)} %get-tuple-element.390) | copy-start | bytes 28
  238.5 9.3 %copy-start.8 = (bf16[1024,256]{1,0:T(8,128)(2,1)S(1)}, bf16[1024,256]{1,0:T(8,128)(2,1)}, u32[]{:S(2)}) copy-start(bf16[1024,256]{1,0:T(8,128)(2,1)} %copy-done.7) | copy-start | bytes 1572868
  238.5 9.3 %copy-start.14 = (s32[1024]{0:T(1024)S(1)}, s32[1024]{0:T(1024)}, u32[]{:S(2)}) copy-start(s32[1024]{0:T(1024)} %param.31) | copy-start | bytes 12292
  238.5 9.3 %copy-start.18 = (f32[1024]{0:T(1024)S(1)}, f32[1024]{0:T(1024)}, u32[]{:S(2)}) copy-start(f32[1024]{0:T(1024)} %copy-done.17) | copy-start | bytes 12292
  243.1 113.4 %copy-start.12 = (f32[256,32]{0,1:T(8,128)S(1)}, f32[256,32]{0,1:T(8,128)}, u32[]{:S(2)}) copy-start(f32[256,32]{0,1:T(8,128)} %copy-done.11) | copy-start | bytes 98308
  247.8 115.6 %copy-start.6 = (f32[1024,256]{1,0:T(8,128)S(1)}, f32[1024,256]{1,0:T(8,128)}, u32[]{:S(2)}) copy-start(f32[1024,256]{1,0:T(8,128)} %copy-done.5) | copy-start | bytes 3145732
  247.8 115.6 %copy-start.16 = (s32[1024]{0:T(1024)S(1)}, s32[1024]{0:T(1024)}, u32[]{:S(2)}) copy-start(s32[1024]{0:T(1024)} %param.30) | copy-start | bytes 12292
  363.4 5.3 copy-start.10
  363.4 6.2 copy-start.22
  371.3 247.3 %all-reduce.7.cloned.1.call-start = ((), (), s32[]{:S(2)}) async-start(), calls=%async_computation.4 | async-start | bytes 1048576 | tf_op jit(solution)/shard_map/psum | solution.py:154
  (7 other events, 13.3 us)
Sparse Core Ops, SparseCore 0:
  130.6 46.4 all-reduce.4
  371.4 198.9 all-reduce.8
  572.7 45.8 all-reduce.6
where the time goes:
time: 628 us; the launch traced here: 627 us
  waiting for transfers between devices  300 us (48%)
  blocking collectives  107 us (17%)
  local copies, waits for them, and re-layouts  77.1 us (12%)
  matrix products  61.4 us (10%)
  starting transfers between devices  33.5 us (5%)
  other arithmetic  33.2 us (5%)
  between operations  14.3 us (2%)
    psum x1, waiting for transfers between devices, shards(): lax.psum((stacked_in, stacked_bias, stacked_out, relation_grad), 'ent')  196 us
    psum x1, blocking collectives, shards(): lax.psum((stacked_in, stacked_bias, stacked_out, relation_grad), 'ent')  107 us
    psum x2, waiting for transfers between devices, shards(): lax.psum(contrib.astype(jnp.bfloat16), 'rel').astype(jnp.float32)  90 us
    all_to_all x2, starting transfers between devices, shards(): lax.all_to_all(picked, 'ent', split_axis=0, concat_axis=0, tiled=True)  21 us
    another operation x3, other arithmetic  18.2 us
    dot_general x4, matrix products, update_backward(): jnp.einsum('nqd,ed->nqe', upstream_low, update_out, preferred_element_typ...  16 us
    all_to_all x2, waiting for transfers between devices, shards(): lax.all_to_all(picked, 'ent', split_axis=0, concat_axis=0, tiled=True)  13.9 us
    dot_general x4, matrix products, update_backward(): jnp.einsum('nqe,nqd->ed', activated, upstream_low, preferred_element_type...  13.9 us
  transfers between devices with their start and end apart: 6, of which 4 were waited for; matrix products, arithmetic and copies ran while one was open for 12% of the time, Pallas kernels for 0%

commit v1 on v0

--- a/solution.py
+++ b/solution.py
@@ -151,7 +151,9 @@
         relation_grad = relation_grad + exact_pick_sum(
             relation_select, weighted * state[edge_source].astype(jnp.float32), 0
         )
-        source_grad = lax.psum(contrib.astype(jnp.bfloat16), "rel").astype(jnp.float32)
+        source_grad = jnp.sum(lax.all_gather(contrib.astype(jnp.bfloat16), "rel"), axis=0).astype(
+            jnp.float32
+        )
         upstream = upstream + grad_state + source_grad
         layer_sums[layer] = sums
     stacked_in = jnp.stack([layer_sums[0][0], layer_sums[1][0]])

time: 628 us -> 481 us (0.77)
  waiting for transfers between devices: 300 us -> 149 us
    psum x1, waiting for transfers between devices: 196 us -> 71.5 us  [shards(): lax.psum((stacked_in, stacked_bias, stacked_out, relation_grad), 'ent')]
    psum x2 -> x0, waiting for transfers between devices: 90 us -> none  [shards(): lax.psum(contrib.astype(jnp.bfloat16), 'rel').astype(jnp.float32)]
    all_gather x0 -> x2, waiting for transfers between devices: none -> 59.8 us  [shards(): lax.all_gather(contrib.astype(jnp.bfloat16), 'rel')]
  transfers between devices with their start and end apart: 6 -> 6, of which waited for: 4 -> 5; matrix products, arithmetic and copies ran while one was open for 12% -> 15% of each run, Pallas kernels for 0% -> 0%
where the time goes in v1:
time: 481 us; the launch traced here: 479 us
  waiting for transfers between devices  149 us (31%)
  blocking collectives  106 us (22%)
  local copies, waits for them, and re-layouts  77.1 us (16%)
  matrix products  61.5 us (13%)
  other arithmetic  37.4 us (8%)
  starting transfers between devices  33.6 us (7%)
  between operations  14.3 us (3%)
    psum x1, blocking collectives, shards(): lax.psum((stacked_in, stacked_bias, stacked_out, relation_grad), 'ent')  106 us
    psum x1, waiting for transfers between devices, shards(): lax.psum((stacked_in, stacked_bias, stacked_out, relation_grad), 'ent')  71.5 us
    all_gather x2, waiting for transfers between devices, shards(): lax.all_gather(contrib.astype(jnp.bfloat16), 'rel')  59.8 us
    all_to_all x2, starting transfers between devices, shards(): lax.all_to_all(picked, 'ent', split_axis=0, concat_axis=0, tiled=True)  21 us
    another operation x3, other arithmetic  18.2 us
    all_to_all x2, waiting for transfers between devices, shards(): lax.all_to_all(picked, 'ent', split_axis=0, concat_axis=0, tiled=True)  17.6 us
    dot_general x4, matrix products, update_backward(): jnp.einsum('nqd,ed->nqe', upstream_low, update_out, preferred_element_typ...  16 us
    dot_general x4, matrix products, update_backward(): jnp.einsum('nqe,nqd->ed', activated, upstream_low, preferred_element_type...  13.9 us
  transfers between devices with their start and end apart: 6, of which 5 were waited for; matrix products, arithmetic and copies ran while one was open for 15% of the time, Pallas kernels for 0%

profile of v1, /device:TPU:2, one launch (start us, length us, event | category | flops | bytes accessed | tf_op | source)
XLA Modules:
  0.0 479.0 jit_solution(56745293016583004)
XLA Ops:
  7.9 18.0 %reduce-window.6 = s32[64,8,128]{2,1,0:T(8,128)S(1)} reduce-window(s32[64,8,128]{2,1,0:T(8,128)S(1)} %fusion.77, s32[]{:T(128)} %constant.27.clone.1), window={size=1x1x128 pad=0_0x0_0x127_0}, to_apply=%region_3.4 | reduce-window | flops 8323072 | bytes 524292 | tf_op jit(solution)/shard_map/reduce-window
  28.0 4.5 scatter_custom_fusion
  33.1 12.0 %all-to-all-start = ((s32[64,1,24]{2,1,0:T(1,128)}), s32[64,1,24]{2,1,0:T(1,128)S(1)}, u32[]{:S(2)}, u32[]{:S(2)}) async-start(s32[64,1,24]{2,1,0:T(1,128)} %bitcast.13), calls=%async_computation | async-start | bytes 65536 | tf_op jit(solution)/shard_map/all_to_all | solution.py:127
  49.7 36.1 %while.38 = (s32[]{:T(128)}, f32[64,256]{1,0:T(8,128)S(1)}, f32[256]{0:T(256)S(1)}, f32[256,32]{0,1:T(8,128)S(1)}, bf16[2,512,256]{2,1,0:T(8,128)(2,1)S(1)}, /*i...) while((s32[]{:T(128)}, f32[64,256]{1,0:T(8,128)S(1)}, ...), condition=%wide.region_2.3_spmd.clone, body=%wide.region_0.2_spmd.clone.sunk | while | flops 556843264 | bytes 33839300 | solution.py:85
  55.6 4.0 fusion.123
  73.7 4.0 fusion.123
  86.0 5.4 %gather_fusion = bf16[1536,256]{1,0:T(8,128)(2,1)} fusion(bf16[1024,256]{1,0:T(8,128)(2,1)S(1)} %bitcast.188, s32[2048]{0:T(1024)S(1)} %pad_clamp_fusion), kind=kCustom, calls=%fused_computation | custom fusion | bytes 1579008 | tf_op jit(solution)/shard_map/gather | solution.py:144
  91.4 10.5 %all-to-all-start.1 = ((bf16[64,24,256]{2,1,0:T(8,128)(2,1)}), bf16[64,24,256]{2,1,0:T(8,128)(2,1)S(1)}, u32[]{:S(2)}, u32[]{:S(2)}) async-start(bf16[64,24,256]{2,1,0:T(8,128)(2,1)} %bitcast.15), calls=%async_computation.1 | async-start | bytes 1572864 | tf_op jit(solution)/shard_map/all_to_all | solution.py:145
  104.7 4.5 gather_fusion.2
  109.8 13.9 %all-to-all-done.1 = bf16[64,24,256]{2,1,0:T(8,128)(2,1)S(1)} async-done(((bf16[64,24,256]{2,1,0:T(8,128)(2,1)}), bf16[64,24,256]{2,1,0:T(8,128)(2,1)S(1)}, u32[]{:S(2)}, u32[]{:S(2)}) %all-to-all-start.1) | async-done | bytes 786464 | tf_op jit(solution)/shard_map/all_to_all | solution.py:145
  123.7 3.9 gather_fusion.1
  130.6 31.7 %all-gather.5.cloned.1.call-done = bf16[4096,256]{1,0:T(8,128)(2,1)} async-done(((bf16[1024,256]{1,0:T(8,128)(2,1)}), bf16[4096,256]{1,0:T(8,128)(2,1)}) %all-gather.5.cloned.1.call-update) | async-done | bytes 2097168 | tf_op jit(solution)/shard_map/all_gather | solution.py:154
  168.0 35.8 %while.39 = (s32[]{:T(128)}, f32[64,256]{1,0:T(8,128)S(1)}, f32[256]{0:T(256)S(1)}, f32[256,32]{0,1:T(8,128)S(1)}, bf16[2,512,256]{2,1,0:T(8,128)(2,1)S(1)}, /*i...) while((s32[]{:T(128)}, f32[64,256]{1,0:T(8,128)S(1)}, ...), condition=%wide.region_11.12_spmd.clone, body=%wide.region_9.11_spmd.clone.sunk | while | flops 556843264 | bytes 33839300 | solution.py:85
  173.9 4.0 fusion.134
  191.8 4.0 fusion.134
  203.8 5.4 %gather_fusion.3 = bf16[1536,256]{1,0:T(8,128)(2,1)} fusion(bf16[1024,256]{1,0:T(8,128)(2,1)S(1)} %bitcast.187, s32[2048]{0:T(1024)S(1)} %pad_clamp_fusion), kind=kCustom, calls=%fused_computation.3 | custom fusion | bytes 1579008 | tf_op jit(solution)/shard_map/gather | solution.py:144
  209.2 10.6 %all-to-all-start.2 = ((bf16[64,24,256]{2,1,0:T(8,128)(2,1)}), bf16[64,24,256]{2,1,0:T(8,128)(2,1)S(1)}, u32[]{:S(2)}, u32[]{:S(2)}) async-start(bf16[64,24,256]{2,1,0:T(8,128)(2,1)} %bitcast.28), calls=%async_computation.2 | async-start | bytes 1572864 | tf_op jit(solution)/shard_map/all_to_all | solution.py:145
  220.0 5.7 %gather_fusion.7 = bf16[1024,256]{1,0:T(8,128)(2,1)} fusion(bf16[1024,256]{1,0:T(8,128)(2,1)} %param.19, s32[1024]{0:T(1024)S(1)} %fusion.78), kind=kCustom, calls=%fused_computation.7 | custom fusion | bytes 1052672 | tf_op jit(solution)/shard_map/gather | solution.py:152
  225.7 4.6 gather_fusion.6
  230.5 4.5 gather_fusion.5
  241.6 4.9 %gather_fusion.4 = bf16[1024,256]{1,0:T(8,128)(2,1)} fusion(bf16[1536,256]{1,0:T(8,128)(2,1)S(1)} %bitcast.200, s32[1024]{0:T(1024)S(1)} %broadcast_clamp_fusion), kind=kCustom, calls=%fused_computation.4 | custom fusion | bytes 1052672 | tf_op jit(solution)/shard_map/gather | solution.py:146
  257.6 105.9 %psum.30 = f32[2,256]{1,0:T(2,128)S(1)} all-reduce(f32[2,256]{1,0:T(2,128)S(1)} %pad_maximum_fusion.8), channel_id=1, replica_groups=mesh['ent'=64,'rel'=4] {'ent'}, use_global_device_ids=true, to_apply=%region_16.17 | all-reduce | flops 512 | bytes 4096 | tf_op jit(solution)/shard_map/psum | solution.py:162
  364.2 71.5 %all-reduce.3.cloned.1.call-done = (f32[328,256]{1,0:T(8,128)}, f32[2,64,256]{2,1,0:T(8,128)}, f32[2,256,32]{1,2,0:T(8,128)}) async-done(((f32[328,256]{1,0:T(8,128)}, f32[2,64,256]{2,1,0:T(8,128)}, f32[2,256,32]{1,2,0:T(8,128)}), (f32[328,256]{1,0:T(8,128)}, f32[2,64,256]{2,1,0:T(8,128)}, f32[2,256,32]{1,2,0:T(8,128)})) %all-reduce.3.cloned.1.call-update) | async-done | bytes 532496 | tf_op jit(solution)/shard_map/psum | solution.py:162
  440.4 28.1 %all-gather.7.cloned.1.call-done = bf16[4096,256]{1,0:T(8,128)(2,1)} async-done(((bf16[1024,256]{1,0:T(8,128)(2,1)}), bf16[4096,256]{1,0:T(8,128)(2,1)}) %all-gather.7.cloned.1.call-update) | async-done | bytes 2097168 | tf_op jit(solution)/shard_map/all_gather | solution.py:154
  (180 shorter events, 102.7 us)
Async XLA Ops:
  7.2 102.1 %copy-start = (bf16[328,256]{1,0:T(8,128)(2,1)S(1)}, bf16[328,256]{1,0:T(8,128)(2,1)}, u32[]{:S(2)}) copy-start(bf16[328,256]{1,0:T(8,128)(2,1)} %param.24) | copy-start | bytes 503812
  33.1 52.7 %all-to-all-start = ((s32[64,1,24]{2,1,0:T(1,128)}), s32[64,1,24]{2,1,0:T(1,128)S(1)}, u32[]{:S(2)}, u32[]{:S(2)}) async-start(s32[64,1,24]{2,1,0:T(1,128)} %bitcast.13), calls=%async_computation | async-start | bytes 65536 | tf_op jit(solution)/shard_map/all_to_all | solution.py:127
  85.9 5.5 %copy-start.11 = (f32[256,32]{0,1:T(8,128)}, f32[256,32]{0,1:T(8,128)S(1)}, u32[]{:S(2)}) copy-start(f32[256,32]{0,1:T(8,128)S(1)} %get-tuple-element.146) | copy-start | bytes 98308
  86.0 16.1 %copy-start.19 = (s32[2,1]{0,1:T(1,128)S(1)}, s32[2,1]{0,1:T(1,128)}, u32[]{:S(2)}) copy-start(s32[2,1]{0,1:T(1,128)} %param.29) | copy-start | bytes 28
  86.0 18.0 %copy-start.20 = (s32[2,2]{1,0:T(2,128)S(1)}, s32[2,2]{1,0:T(2,128)}, u32[]{:S(2)}) copy-start(s32[2,2]{1,0:T(2,128)} %param.28) | copy-start | bytes 52
  86.0 18.7 %copy-start.15 = (s32[1024]{0:T(1024)S(1)}, s32[1024]{0:T(1024)}, u32[]{:S(2)}) copy-start(s32[1024]{0:T(1024)} %param.30) | copy-start | bytes 12292
  91.4 17.9 %copy-start.13 = (s32[1024]{0:T(1024)S(1)}, s32[1024]{0:T(1024)}, u32[]{:S(2)}) copy-start(s32[1024]{0:T(1024)} %param.31) | copy-start | bytes 12292
  91.4 32.3 %all-to-all-start.1 = ((bf16[64,24,256]{2,1,0:T(8,128)(2,1)}), bf16[64,24,256]{2,1,0:T(8,128)(2,1)S(1)}, u32[]{:S(2)}, u32[]{:S(2)}) async-start(bf16[64,24,256]{2,1,0:T(8,128)(2,1)} %bitcast.15), calls=%async_computation.1 | async-start | bytes 1572864 | tf_op jit(solution)/shard_map/all_to_all | solution.py:145
  101.9 60.4 %all-gather.5.cloned.1.call-start = ((), (), s32[]{:S(2)}) async-start(), calls=%async_computation.3 | async-start | bytes 2621440 | tf_op jit(solution)/shard_map/all_gather | solution.py:154
  109.2 19.4 %copy-start.17 = (f32[1024]{0:T(1024)}, f32[1024]{0:T(1024)S(1)}, u32[]{:S(2)}) copy-start(f32[1024]{0:T(1024)S(1)} %gather_fusion.2) | copy-start | bytes 12292
  109.8 18.9 %copy-start.5 = (f32[1024,256]{1,0:T(8,128)}, f32[1024,256]{1,0:T(8,128)S(1)}, u32[]{:S(2)}) copy-start(f32[1024,256]{1,0:T(8,128)S(1)} %fusion.40) | copy-start | bytes 3145732
  128.7 35.7 %copy-start.4 = (f32[2,512,256]{2,1,0:T(8,128)S(1)}, f32[2,512,256]{2,1,0:T(8,128)}, u32[]{:S(2)}) copy-start(f32[2,512,256]{2,1,0:T(8,128)} %get-tuple-element.137) | copy-start | bytes 3145732
  209.2 32.5 %all-to-all-start.2 = ((bf16[64,24,256]{2,1,0:T(8,128)(2,1)}), bf16[64,24,256]{2,1,0:T(8,128)(2,1)S(1)}, u32[]{:S(2)}, u32[]{:S(2)}) async-start(bf16[64,24,256]{2,1,0:T(8,128)(2,1)} %bitcast.28), calls=%async_computation.2 | async-start | bytes 1572864 | tf_op jit(solution)/shard_map/all_to_all | solution.py:145
  219.8 10.6 %copy-start.21 = (pred[8]{0:T(512)(128)(4,1)S(1)}, pred[8]{0:T(512)(128)(4,1)}, u32[]{:S(2)}) copy-start(pred[8]{0:T(512)(128)(4,1)} %get-tuple-element.390) | copy-start | bytes 28
  219.8 215.9 %all-reduce.3.cloned.1.call-start = ((), (), s32[]{:S(2)}) async-start(), calls=%async_computation.5 | async-start | bytes 1064960 | tf_op jit(solution)/shard_map/psum | solution.py:162
  225.7 9.3 %copy-start.8 = (bf16[1024,256]{1,0:T(8,128)(2,1)S(1)}, bf16[1024,256]{1,0:T(8,128)(2,1)}, u32[]{:S(2)}) copy-start(bf16[1024,256]{1,0:T(8,128)(2,1)} %copy-done.7) | copy-start | bytes 1572868
  225.7 9.3 %copy-start.14 = (s32[1024]{0:T(1024)S(1)}, s32[1024]{0:T(1024)}, u32[]{:S(2)}) copy-start(s32[1024]{0:T(1024)} %param.31) | copy-start | bytes 12292
  225.7 9.3 %copy-start.18 = (f32[1024]{0:T(1024)S(1)}, f32[1024]{0:T(1024)}, u32[]{:S(2)}) copy-start(f32[1024]{0:T(1024)} %copy-done.17) | copy-start | bytes 12292
  230.4 6.4 %copy-start.12 = (f32[256,32]{0,1:T(8,128)S(1)}, f32[256,32]{0,1:T(8,128)}, u32[]{:S(2)}) copy-start(f32[256,32]{0,1:T(8,128)} %copy-done.11) | copy-start | bytes 98308
  235.0 11.6 %copy-start.6 = (f32[1024,256]{1,0:T(8,128)S(1)}, f32[1024,256]{1,0:T(8,128)}, u32[]{:S(2)}) copy-start(f32[1024,256]{1,0:T(8,128)} %copy-done.5) | copy-start | bytes 3145732
  235.0 11.5 %copy-start.16 = (s32[1024]{0:T(1024)S(1)}, s32[1024]{0:T(1024)}, u32[]{:S(2)}) copy-start(s32[1024]{0:T(1024)} %param.30) | copy-start | bytes 12292
  246.6 5.3 %copy-start.10 = (bf16[1024,256]{1,0:T(8,128)(2,1)S(1)}, bf16[1024,256]{1,0:T(8,128)(2,1)}, u32[]{:S(2)}) copy-start(bf16[1024,256]{1,0:T(8,128)(2,1)} %gather_fusion.7) | copy-start | bytes 1572868
  246.6 6.2 %copy-start.22 = (f32[328,256]{1,0:T(8,128)S(1)}, f32[328,256]{1,0:T(8,128)}, u32[]{:S(2)}) copy-start(f32[328,256]{1,0:T(8,128)} %fusion.38) | copy-start | bytes 1007620
  254.5 214.0 %all-gather.7.cloned.1.call-start = ((), (), s32[]{:S(2)}) async-start(), calls=%async_computation.4 | async-start | bytes 2621440 | tf_op jit(solution)/shard_map/all_gather | solution.py:154
  (7 other events, 13.3 us)
Sparse Core Ops, SparseCore 0:
  130.6 31.5 all-gather.4
  254.6 180.9 all-reduce.2
  437.5 31.0 all-gather.6
